TPU v7x, 32 devices: a whole 2x2x4 slice. The times are simulated.
32 devices in a mesh: group: 2 (over x), tm: 4 (over y, core), inline: 4 (over z).
Axes of the slice: x: 2, y: 2, z: 4, core: 2. Of those that a mesh axis runs over, the one named last changes fastest.
Arguments:
- near_trace: float32 [128, 512], P(('group', 'inline'), 'tm'), parts along dimension 0, may hold values from -1.5 to 1.5
- far_trace: float32 [128, 512], P(('group', 'inline'), 'tm'), parts along dimension 0, may hold values from -1.5 to 1.5
- inline_weight: int32 [128, 512], P(('group', 'inline'), 'tm'), parts along dimension 0, may hold values from 0 to 15
- time_weight: int32 [128, 512], P(('group', 'inline'), 'tm'), parts along dimension 0, may hold values from 0 to 15
- lag_low: int32 [128], P(('group', 'inline')), parts along dimension 0, may hold values from 0 to 15
- lag_high: int32 [128], P(('group', 'inline')), parts along dimension 0, may hold values from 48 to 63
- strain: int32 [16], P(('group', 'tm')), parts along dimension 0, may hold values from 1 to 3
Outputs:
- accumulated: float32 [64, 128, 512], P(None, ('group', 'inline'), 'tm'), parts along dimension 1
There are 2 independent parts, one for each index of `group`. A program takes and returns all parts, laid end to end along the dimension named above; each array names one. Nothing has to cross between parts.
All inputs are finite; a program needn't handle non-finite values.
Results may differ from a plain program's by a relative error of at most 0.0003.
Values sent between devices are 32-bit elements; how exact they have to be, the bound alone decides.
A program may use at most 64 MiB of HBM per device.

v0:
```python
import functools

import jax
import jax.numpy as jnp
from jax import lax
from jax.experimental import pallas as pl
from jax.experimental.pallas import tpu as pltpu
from jax.sharding import PartitionSpec as P

L = 64
STRETCH = 64
ITERS = 10

BIG = 1000000000.0
PENALTY = 2.0
FACE_SCALE = 0.016

SUB = 8
LANES = 128


def neighbours(cells, axis):
    count = lax.axis_size(axis)
    ends = count - 1
    before = lax.ppermute(cells, axis, [(i, i + 1) for i in range(ends)])
    after = lax.ppermute(cells, axis, [(i + 1, i) for i in range(ends)])
    return before, after


def segments(width, reach, chunk_len):
    cuts = {0, width}
    cuts |= set(range(0, width, STRETCH))
    cuts |= {c * chunk_len - reach for c in range(1, -(-(width + reach) // chunk_len))}
    cuts = sorted(x for x in cuts if 0 <= x <= width)
    return list(zip(cuts[:-1], cuts[1:]))


def kernel(
    dims,
    far_ref,
    near_ref,
    a_ref,
    b_ref,
    bounds_ref,
    strain_ref,
    out_ref,
    m_ref,
    y_ref,
    low_ref,
    send_ref,
    recv_ref,
    send_sem,
    recv_sem,
):
    rows, width, reach, pitch, chunks, chunk_len, count = dims
    groups = L // SUB
    me = lax.axis_index("tm")
    barrier = pltpu.get_barrier_semaphore()

    @pl.when(me > 0)
    def _():
        pl.semaphore_signal(
            barrier, inc=1, device_id={"tm": me - 1}, device_id_type=pl.DeviceIdType.MESH
        )

    @pl.when(me < count - 1)
    def _():
        pl.semaphore_wait(barrier, 1)

    lane_low = bounds_ref[0:1, :]
    lane_high = bounds_ref[1:2, :]
    sub = lax.broadcasted_iota(jnp.int32, (SUB, LANES), 0)
    extra = []
    for v in range(groups):
        lag = (sub * groups + v).astype(jnp.float32)
        extra.append(jnp.where((lag < lane_low) | (lag > lane_high), PENALTY, 0.0))

    def build(j, carry):
        near = near_ref[pl.ds(j, 1), :]
        for v in range(groups):
            shifted = far_ref[pl.ds(j + v, SUB, stride=groups), :]
            diff = near - shifted
            m_ref[j, v] = diff * diff + extra[v]
        return carry

    lax.fori_loop(0, chunk_len, build, 0, unroll=2)

    last = chunk_len - 1

    def sweep(k, carry):
        first = [m_ref[0, v] for v in range(groups)]
        final = [m_ref[last, v] for v in range(groups)]
        b_last = b_ref[pl.ds(last, 1), :]
        flux = []
        for v in range(groups):
            wrapped = pltpu.roll(first[v], LANES - pitch, 1)
            m_ref[chunk_len, v] = wrapped
            flux.append(pltpu.roll(b_last * (wrapped - final[v]), pitch, 1))

        def cell(j, state):
            here, before = state
            a_row = a_ref[pl.ds(j, 1), :]
            b_row = b_ref[pl.ds(j, 1), :]
            nexts, fluxes = [], []
            for v in range(groups):
                centre = here[v]
                ahead = m_ref[j + 1, v]
                side = a_row * (pltpu.roll(centre, LANES - 1, 1) - centre)
                along = b_row * (ahead - centre)
                m_ref[j, v] = ((centre + side) - pltpu.roll(side, 1, 1)) + (along - before[v])
                nexts.append(ahead)
                fluxes.append(along)
            return nexts, fluxes

        lax.fori_loop(0, chunk_len, cell, (first, flux), unroll=2)
        return carry

    lax.fori_loop(0, ITERS, sweep, 0)

    recv_copy = pltpu.make_async_remote_copy(
        src_ref=send_ref,
        dst_ref=recv_ref,
        send_sem=send_sem,
        recv_sem=recv_sem,
        device_id={"tm": lax.min(me + 1, count - 1)},
        device_id_type=pl.DeviceIdType.MESH,
    )

    @pl.when(me == 0)
    def _():
        recv_ref[...] = jnp.zeros(recv_ref.shape, jnp.float32)

    @pl.when(me > 0)
    def _():
        recv_copy.wait_recv()

    state = [recv_ref[v] for v in range(groups)]
    lane = lax.broadcasted_iota(jnp.int32, (SUB, LANES), 1)
    at_low = sub == 0
    at_high = sub == SUB - 1
    chunk_now = 0
    for start, stop in segments(width, reach, chunk_len):
        chunk = (start + reach) // chunk_len
        if chunk != chunk_now:
            state = [pltpu.roll(x, pitch, 1) for x in state]
            chunk_now = chunk
        radius = strain_ref[start // STRETCH]
        gate2 = jnp.full((SUB, LANES), jnp.where(radius >= 2, -BIG, BIG), jnp.float32)
        gate3 = jnp.full((SUB, LANES), jnp.where(radius >= 3, -BIG, BIG), jnp.float32)
        mine = (lane >= chunk * pitch) & (lane < (chunk + 1) * pitch)

        def advance(j, x):
            wide = {v: x[v] for v in range(groups)}
            for k in range(1, 4):
                wide[-k] = jnp.where(at_low, BIG, pltpu.roll(x[groups - k], 1, 0))
                wide[groups - 1 + k] = jnp.where(at_high, BIG, pltpu.roll(x[k - 1], SUB - 1, 0))
            pair = {v: jnp.minimum(wide[v], wide[v + 1]) for v in range(-1, groups)}
            new = []
            for v in range(groups):
                near3 = jnp.minimum(pair[v - 1], pair[v])
                two = jnp.maximum(jnp.minimum(wide[v - 2], wide[v + 2]), gate2)
                three = jnp.maximum(jnp.minimum(wide[v - 3], wide[v + 3]), gate3)
                total = m_ref[j, v] + jnp.minimum(near3, jnp.minimum(two, three))
                if chunk == 0:
                    y_ref[j, v] = total
                else:
                    y_ref[j, v] = jnp.where(mine, total, y_ref[j, v])
                new.append(total)
            return new

        base = chunk * chunk_len - reach
        state = lax.fori_loop(start - base, stop - base, advance, state, unroll=2)

    @pl.when(me < count - 1)
    def _():
        for v in range(groups):
            send_ref[v] = pltpu.roll(state[v], (LANES - chunk_now * pitch) % LANES, 1)
        recv_copy.start()

    def least(j, carry):
        low = y_ref[j, 0]
        for v in range(1, groups):
            low = jnp.minimum(low, y_ref[j, v])
        low = jnp.min(low, axis=0, keepdims=True)
        low_ref[pl.ds(j, 1), :] = low
        return carry

    lax.fori_loop(0, chunk_len, least, 0, unroll=2)

    def emit(lag, carry):
        sub_index, v = lag // groups, lag % groups
        cells = y_ref[0:chunk_len, v, sub_index, :] - low_ref[0:chunk_len, :]
        flat = jnp.transpose(cells)
        parts = []
        for c in range(chunks):
            begin = max(reach - c * chunk_len, 0)
            end = min(width + reach - c * chunk_len, chunk_len)
            if end > begin:
                parts.append(flat[c * pitch + reach : c * pitch + reach + rows, begin:end])
        out_ref[lag] = jnp.concatenate(parts, axis=1)
        return carry

    for lag in range(L):
        emit(lag, 0)

    @pl.when(me < count - 1)
    def _():
        recv_copy.wait_send()


def per_device(near_trace, far_trace, inline_weight, time_weight, lag_low, lag_high, strain):
    rows, width = near_trace.shape
    half = L // 2
    reach = ITERS
    groups = L // SUB
    total_rows = rows + 2 * reach
    chunks = LANES // total_rows
    pitch = LANES // chunks
    total_cols = width + 2 * reach
    chunk_len = -(-total_cols // chunks)
    count = lax.axis_size("tm")

    fields = jnp.stack(
        [
            far_trace,
            near_trace,
            inline_weight.astype(jnp.float32),
            time_weight.astype(jnp.float32),
        ]
    )
    before, after = neighbours(fields, "tm")
    deep = half + reach
    wide = jnp.concatenate([before[:, :, width - deep :], fields, after[:, :, :deep]], axis=2)
    bounds = jnp.stack([lag_low, lag_high], axis=-1).astype(jnp.float32)
    marks = jnp.zeros((1, rows, wide.shape[2]), jnp.float32).at[0, :, :2].set(bounds)
    wide = jnp.concatenate([wide, marks], axis=0)
    count_in = lax.axis_size("inline")
    up = lax.ppermute(
        wide[:, rows - reach :], "inline", [(i, i + 1) for i in range(count_in - 1)]
    )
    down = lax.ppermute(wide[:, :reach], "inline", [(i + 1, i) for i in range(count_in - 1)])
    wide = jnp.concatenate([up, wide, down], axis=1)

    def packed(cells, length):
        need = (chunks - 1) * chunk_len + length
        cells = jnp.pad(
            cells, ((0, pitch - total_rows), (0, max(need - cells.shape[1], 0)))
        )
        lanes = jnp.concatenate(
            [cells[:, c * chunk_len : c * chunk_len + length] for c in range(chunks)], axis=0
        )
        lanes = jnp.pad(lanes, ((0, LANES - lanes.shape[0]), (0, -length % SUB)))
        return jnp.transpose(lanes)

    core = wide[:, :, half : half + total_cols]
    far_p = packed(wide[0], chunk_len + L)
    near_p = packed(core[1], chunk_len)
    inline_w, time_w = core[2], core[3]
    a_face = FACE_SCALE * jnp.minimum(inline_w, jnp.pad(inline_w[1:], ((0, 1), (0, 0))))
    b_face = FACE_SCALE * jnp.minimum(time_w, jnp.pad(time_w[:, 1:], ((0, 0), (0, 1))))
    a_p = packed(a_face, chunk_len)
    b_p = packed(b_face, chunk_len)
    line = jnp.pad(wide[4, :, :2], ((0, pitch - total_rows), (0, 0)))
    line = jnp.pad(jnp.tile(line, (chunks, 1)), ((0, LANES - chunks * pitch), (0, SUB - 2)))
    bounds_p = jnp.transpose(line)

    vmem = pl.BlockSpec(memory_space=pltpu.VMEM)
    dims = (rows, width, reach, pitch, chunks, chunk_len, count)
    padded_len = -(-chunk_len // SUB) * SUB
    return pl.pallas_call(
        functools.partial(kernel, dims),
        out_shape=jax.ShapeDtypeStruct((L, rows, width), jnp.float32),
        in_specs=[vmem] * 5 + [pl.BlockSpec(memory_space=pltpu.SMEM)],
        out_specs=vmem,
        scratch_shapes=[
            pltpu.VMEM((chunk_len + 1, groups, SUB, LANES), jnp.float32),
            pltpu.VMEM((padded_len, groups, SUB, LANES), jnp.float32),
            pltpu.VMEM((padded_len, LANES), jnp.float32),
            pltpu.VMEM((groups, SUB, LANES), jnp.float32),
            pltpu.VMEM((groups, SUB, LANES), jnp.float32),
            pltpu.SemaphoreType.DMA,
            pltpu.SemaphoreType.DMA,
        ],
        compiler_params=pltpu.CompilerParams(collective_id=0, has_side_effects=True),
    )(far_p, near_p, a_p, b_p, bounds_p, strain)


def solution(mesh):
    return jax.shard_map(
        per_device,
        mesh=mesh,
        in_specs=(
            P(("group", "inline"), "tm"),
            P(("group", "inline"), "tm"),
            P(("group", "inline"), "tm"),
            P(("group", "inline"), "tm"),
            P(("group", "inline")),
            P(("group", "inline")),
            P(("group", "tm")),
        ),
        out_specs=P(None, ("group", "inline"), "tm"),
        check_vma=False,
    )
```

profile of v0, /device:TPU:5, one launch (start us, length us, event | category | flops | bytes accessed | tf_op | source)
XLA Modules:
  0.0 81.8 jit_solution(4948053593396549731)
XLA Ops:
  0.0 0.7 convert_bitcast_fusion
  0.8 2.6 %collective-permute-start.1 = (f32[4,16,128]{2,1,0:T(8,128)S(1)}, f32[4,16,128]{2,1,0:T(8,128)S(1)}, u32[]{:S(2)}, u32[]{:S(2)}) collective-permute-start(f32[4,16,128]{2,1,0:T(8,128)S(1)} %pad_maximum_fusion.2), channel_id=1, source_target_pairs={{4,0},{8,4},{12,8},{5,1},{9,5},{13,9},{6,2},{10,6},{14,10},{7,3},{... | collective-permute-start | bytes 98312 | tf_op jit(solution)/shard_map/ppermute | solution.py:26
  3.4 1.3 %collective-permute-start = (f32[4,16,128]{2,1,0:T(8,128)S(1)}, f32[4,16,128]{2,1,0:T(8,128)S(1)}, u32[]{:S(2)}, u32[]{:S(2)}) collective-permute-start(f32[4,16,128]{2,1,0:T(8,128)S(1)} %pad_maximum_fusion.2), channel_id=1, source_target_pairs={{0,4},{4,8},{8,12},{1,5},{5,9},{9,13},{2,6},{6,10},{10,14},{3,7},{... | collective-permute-start | bytes 98312 | tf_op jit(solution)/shard_map/ppermute | solution.py:25
  4.7 0.6 copy-done.3
  5.4 1.0 %collective-permute-done = f32[4,16,128]{2,1,0:T(8,128)S(1)} collective-permute-done((f32[4,16,128]{2,1,0:T(8,128)S(1)}, f32[4,16,128]{2,1,0:T(8,128)S(1)}, u32[]{:S(2)}, u32[]{:S(2)}) %collective-permute-start) | collective-permute-done | bytes 32800 | tf_op jit(solution)/shard_map/ppermute | solution.py:25
  6.7 3.2 %collective-permute-start.2 = (f32[5,10,212]{2,1,0:T(8,128)S(1)}, f32[5,10,212]{2,1,0:T(8,128)S(1)}, u32[]{:S(2)}, u32[]{:S(2)}) collective-permute-start(f32[5,10,212]{2,1,0:T(8,128)S(1)} %get-tuple-element.23), channel_id=1, source_target_pairs={{0,1},{1,2},{2,3},{4,5},{5,6},{6,7},{8,9},{9,10},{10,11},{12,13},{... | collective-permute-start | bytes 127208 | tf_op jit(solution)/shard_map/ppermute | solution.py:238
  9.9 1.3 %collective-permute-start.3 = (f32[5,10,212]{2,1,0:T(8,128)S(1)}, f32[5,10,212]{2,1,0:T(8,128)S(1)}, u32[]{:S(2)}, u32[]{:S(2)}) collective-permute-start(f32[5,10,212]{2,1,0:T(8,128)S(1)} %get-tuple-element.24), channel_id=1, source_target_pairs={{1,0},{2,1},{3,2},{5,4},{6,5},{7,6},{9,8},{10,9},{11,10},{13,12},{... | collective-permute-start | bytes 127208 | tf_op jit(solution)/shard_map/ppermute | solution.py:241
  11.2 0.2 collective-permute-done.2
  11.3 3.7 %collective-permute-done.3 = f32[5,10,212]{2,1,0:T(8,128)S(1)} collective-permute-done((f32[5,10,212]{2,1,0:T(8,128)S(1)}, f32[5,10,212]{2,1,0:T(8,128)S(1)}, u32[]{:S(2)}, u32[]{:S(2)}) %collective-permute-start.3) | collective-permute-done | bytes 42432 | tf_op jit(solution)/shard_map/ppermute | solution.py:241
  15.1 0.1 pad_maximum_fusion
  15.3 0.6 copy-done
  16.1 0.6 pad_bitcast_fusion.bounds_ref
  16.7 0.1 copy.26
  16.8 0.1 copy.27
  16.9 0.7 slice-done
  17.6 0.1 copy.23
  17.8 0.1 copy.25
  17.9 0.1 copy.24
  18.1 0.7 fusion.1.far_ref
  18.8 0.7 fusion.2.b_ref
  19.5 0.7 fusion.3.a_ref
  20.2 0.7 fusion.4.near_ref
  20.9 59.0 %shard_map.73 = f32[64,16,128]{2,1,0:T(8,128)} custom-call(f32[120,128]{1,0:T(8,128)} %fusion.1.far_ref, f32[56,128]{1,0:T(8,128)} %fusion.4.near_ref, f32[56,128]{1,0:T(8,128)} %fusion.3.a_ref, f32[56,128]{1,0:T(8,128)} %fusion.2.b_ref, f32[8,128]{1,0:T(8,128)} %pad_bitcast_fusion.bounds_ref, s32[2]{0:T(128)} %strain_ref.1), custom_call_target="tpu_custom_call" | custom-call | tf_op jit(solution)/shard_map/pallas_call | solution.py:270
  79.9 1.9 %copy.30 = f32[64,16,128]{2,1,0:T(8,128)} copy(f32[64,16,128]{2,1,0:T(8,128)} %shard_map.73) | data formatting | bytes 1048576
  (31 shorter events, 0.8 us)
Async XLA Ops:
  0.0 0.7 copy-start.1
  0.0 0.8 copy-start.2
  0.8 5.8 %collective-permute-start.1 = (f32[4,16,128]{2,1,0:T(8,128)S(1)}, f32[4,16,128]{2,1,0:T(8,128)S(1)}, u32[]{:S(2)}, u32[]{:S(2)}) collective-permute-start(f32[4,16,128]{2,1,0:T(8,128)S(1)} %pad_maximum_fusion.2), channel_id=1, source_target_pairs={{4,0},{8,4},{12,8},{5,1},{9,5},{13,9},{6,2},{10,6},{14,10},{7,3},{... | collective-permute-start | bytes 98312 | tf_op jit(solution)/shard_map/ppermute | solution.py:26
  3.4 3.1 %collective-permute-start = (f32[4,16,128]{2,1,0:T(8,128)S(1)}, f32[4,16,128]{2,1,0:T(8,128)S(1)}, u32[]{:S(2)}, u32[]{:S(2)}) collective-permute-start(f32[4,16,128]{2,1,0:T(8,128)S(1)} %pad_maximum_fusion.2), channel_id=1, source_target_pairs={{0,4},{4,8},{8,12},{1,5},{5,9},{9,13},{2,6},{6,10},{10,14},{3,7},{... | collective-permute-start | bytes 98312 | tf_op jit(solution)/shard_map/ppermute | solution.py:25
  4.7 0.7 copy-start.3
  4.7 0.7 copy-start.4
  6.7 4.7 %collective-permute-start.2 = (f32[5,10,212]{2,1,0:T(8,128)S(1)}, f32[5,10,212]{2,1,0:T(8,128)S(1)}, u32[]{:S(2)}, u32[]{:S(2)}) collective-permute-start(f32[5,10,212]{2,1,0:T(8,128)S(1)} %get-tuple-element.23), channel_id=1, source_target_pairs={{0,1},{1,2},{2,3},{4,5},{5,6},{6,7},{8,9},{9,10},{10,11},{12,13},{... | collective-permute-start | bytes 127208 | tf_op jit(solution)/shard_map/ppermute | solution.py:238
  9.9 5.2 %collective-permute-start.3 = (f32[5,10,212]{2,1,0:T(8,128)S(1)}, f32[5,10,212]{2,1,0:T(8,128)S(1)}, u32[]{:S(2)}, u32[]{:S(2)}) collective-permute-start(f32[5,10,212]{2,1,0:T(8,128)S(1)} %get-tuple-element.24), channel_id=1, source_target_pairs={{1,0},{2,1},{3,2},{5,4},{6,5},{7,6},{9,8},{10,9},{11,10},{13,12},{... | collective-permute-start | bytes 127208 | tf_op jit(solution)/shard_map/ppermute | solution.py:241
  15.2 0.7 copy-start
  16.8 0.8 slice-start
where the time goes:
time: 82.2 us; the launch traced here: 81.8 us
  Pallas kernels  59 us (72%)
  starting transfers between devices  8.37 us (10%)
  local copies, waits for them, and re-layouts  5.52 us (7%)
  waiting for transfers between devices  4.91 us (6%)
  other arithmetic  3.78 us (5%)
    pallas_call x1, Pallas kernels, per_device(): pl.pallas_call(functools.partial(kernel, dims), out_shape=jax.ShapeDtypeS...  59 us
    unnamed x17, local copies, waits for them, and re-layouts  3.74 us
    ppermute x1, waiting for transfers between devices, per_device(): lax.ppermute(wide[:, :reach], 'inline', [(i + 1, i) for i in range(count_...  3.72 us
    ppermute x1, starting transfers between devices, per_device(): lax.ppermute(wide[:, rows - reach:], 'inline', [(i, i + 1) for i in range...  3.2 us
    transpose x4, other arithmetic, packed(): return jnp.transpose(lanes)  2.79 us
    ppermute x1, starting transfers between devices, neighbours(): after = lax.ppermute(cells, axis, [(i + 1, i) for i in range(ends)])  2.58 us
  transfers between devices with their start and end apart: 4, of which 3 were waited for; matrix products, arithmetic and copies ran while one was open for 0% of the time, Pallas kernels for 0%

commit v1 on v0

v1 whole, which is shorter than its diff:
```python
import functools

import jax
import jax.numpy as jnp
from jax import lax
from jax.experimental import pallas as pl
from jax.experimental.pallas import tpu as pltpu
from jax.sharding import PartitionSpec as P

L = 64
STRETCH = 64
ITERS = 10

BIG = 1000000000.0
PENALTY = 2.0
FACE_SCALE = 0.016

SUB = 8
LANES = 128


def segments(width, reach, chunk_len):
    cuts = {0, width}
    cuts |= set(range(0, width, STRETCH))
    cuts |= {c * chunk_len - reach for c in range(1, -(-(width + reach) // chunk_len))}
    cuts = sorted(x for x in cuts if 0 <= x <= width)
    return list(zip(cuts[:-1], cuts[1:]))


OFFSETS = [(di, dj) for di in (-1, 0, 1) for dj in (-1, 0, 1) if (di, dj) != (0, 0)]


def slot_of(di, dj):
    return (di + 1) * 3 + dj + 1


def kernel(
    dims,
    fields_ref,
    strain_ref,
    out_ref,
    recv_ref,
    time_ref,
    far_ref,
    near_ref,
    face_ref,
    m_ref,
    y_ref,
    low_ref,
    send_ref,
    enter_ref,
    send_sems,
    recv_sems,
    send_sem,
    recv_sem,
):
    rows, width, reach, classes, own, side_pairs, pitch, chunks, chunk_len, count, count_in = dims
    groups = L // SUB
    half = L // 2
    me = lax.axis_index("tm")
    here_in = lax.axis_index("inline")

    def present(di, dj):
        ok = None
        for step, place, total in ((di, here_in, count_in), (dj, me, count)):
            if step:
                inside = (place + step >= 0) & (place + step < total)
                ok = inside if ok is None else ok & inside
        return ok

    def device(di, dj):
        return {
            "inline": lax.clamp(0, here_in + di, count_in - 1),
            "tm": lax.clamp(0, me + dj, count - 1),
        }

    barrier = pltpu.get_barrier_semaphore()
    for di, dj in OFFSETS:

        @pl.when(present(di, dj))
        def _():
            pl.semaphore_signal(
                barrier, inc=1, device_id=device(di, dj), device_id_type=pl.DeviceIdType.MESH
            )

    beside = [
        1 + (place > 0).astype(jnp.int32) + (place < total - 1).astype(jnp.int32)
        for place, total in ((here_in, count_in), (me, count))
    ]
    pl.semaphore_wait(barrier, beside[0] * beside[1] - 1)

    def halo_copy(di, dj):
        target = slot_of(-di, -dj)
        return pltpu.make_async_remote_copy(
            src_ref=fields_ref,
            dst_ref=recv_ref.at[target],
            send_sem=send_sems.at[slot_of(di, dj)],
            recv_sem=recv_sems.at[target],
            device_id=device(di, dj),
            device_id_type=pl.DeviceIdType.MESH,
        )

    for di, dj in OFFSETS:

        @pl.when(present(di, dj))
        def _():
            halo_copy(di, dj).start()

        @pl.when(jnp.logical_not(present(di, dj)))
        def _():
            recv_ref[slot_of(di, dj)] = jnp.zeros(fields_ref.shape, jnp.float32)

    for di, dj in OFFSETS:

        @pl.when(present(di, dj))
        def _():
            halo_copy(-di, -dj).wait_recv()

    stacked = 3 * own

    def block(field, dj, parity):
        parts = []
        for di in (-1, 0, 1):
            pick = pl.ds(parity, own, stride=classes)
            if di == 0 and dj == 0:
                parts.append(fields_ref[field, pick, :])
            else:
                parts.append(recv_ref[slot_of(di, dj), field, pick, :])
        return parts

    for pair in range(2):
        for dj in (-1, 0, 1):
            parts = []
            for field in (2 * pair, 2 * pair + 1):
                for parity in range(classes):
                    parts += block(field, dj, parity)
            tall = jnp.concatenate(parts, axis=0)
            time_ref[pair, (dj + 1) * width : (dj + 2) * width, 0 : tall.shape[0]] = (
                jnp.transpose(tall)
            )

    line = lax.broadcasted_iota(jnp.int32, (1, LANES), 1)
    spot = line % pitch
    live = line < chunks * pitch
    first_time = width - reach

    def pack(pair, start, length, lane_off, step):
        size = -(-length // SUB) * SUB
        result = None
        for c in range(chunks):
            base = start + c * step
            x = time_ref[pair, base : base + size, :]
            x = pltpu.roll(x, (c * pitch - lane_off) % LANES, 1)
            result = x if c == 0 else jnp.where(line >= c * pitch, x, result)
        return jnp.where(live, result, 0.0), size

    skip = own - side_pairs
    span = own + 2 * side_pairs
    inline_rows = []
    for e in range(classes):
        far, size = pack(0, first_time - half, chunk_len + L, e * stacked + skip, chunk_len)
        far_ref[e, 0:size] = far
        near, size = pack(
            0, first_time, chunk_len, (classes + e) * stacked + skip, chunk_len
        )
        near_ref[e, 0:size] = near
        inline_rows.append(pack(1, first_time, chunk_len, e * stacked + skip, chunk_len)[0])
        time_off = (classes + e) * stacked + skip
        time_now = pack(1, first_time, chunk_len, time_off, chunk_len)[0]
        time_next = pack(1, first_time + 1, chunk_len, time_off, chunk_len)[0]
        face_ref[classes + 1 + e, 0:size] = FACE_SCALE * jnp.minimum(time_now, time_next)
    for e in range(classes):
        if e < classes - 1:
            other, inner = inline_rows[e + 1], span
        else:
            other, inner = pltpu.roll(inline_rows[0], LANES - 1, 1), span - 1
        face = jnp.where(spot < inner, FACE_SCALE * jnp.minimum(inline_rows[e], other), 0.0)
        face = jnp.where(live, face, 0.0)
        face_ref[e, 0:size] = face
        if e == classes - 1:
            face_ref[classes, 0:size] = pltpu.roll(face, 1, 1)

    sub = lax.broadcasted_iota(jnp.int32, (SUB, LANES), 0)
    extra = []
    for e in range(classes):
        marks = jnp.transpose(jnp.concatenate(block(4, 0, e) * 2, axis=0))[0:SUB]
        marks = jnp.concatenate(
            [marks, jnp.zeros((SUB, LANES - marks.shape[1]), jnp.float32)], axis=1
        )
        bounds = None
        for c in range(chunks):
            x = pltpu.roll(marks, (c * pitch - skip) % LANES, 1)
            bounds = x if c == 0 else jnp.where(line >= c * pitch, x, bounds)
        lane_low, lane_high = bounds[0:1], bounds[1:2]
        for v in range(groups):
            lag = (sub * groups + v).astype(jnp.float32)
            extra.append(jnp.where((lag < lane_low) | (lag > lane_high), PENALTY, 0.0))

    for e in range(classes):

        def build(j, carry):
            near = near_ref[e, pl.ds(j, 1), :]
            for v in range(groups):
                shifted = far_ref[e, pl.ds(j + v, SUB, stride=groups), :]
                diff = near - shifted
                m_ref[e, j, v] = diff * diff + extra[e * groups + v]
            return carry

        lax.fori_loop(0, chunk_len, build, 0, unroll=5)

    last = chunk_len - 1

    def sweep(k, carry):
        for begin in range(0, groups, 4):
            picks = [(e, v) for e in range(classes) for v in range(begin, begin + 4)]
            first = {p: m_ref[p[0], 0, p[1]] for p in picks}
            flux = {}
            for p in picks:
                e, v = p
                wrapped = pltpu.roll(first[p], LANES - pitch, 1)
                m_ref[e, chunk_len, v] = wrapped
                b_last = face_ref[classes + 1 + e, pl.ds(last, 1), :]
                flux[p] = pltpu.roll(b_last * (wrapped - m_ref[e, last, v]), pitch, 1)

            def cell(j, state):
                here, before = state
                here = dict(zip(picks, here))
                before = dict(zip(picks, before))
                a_rows = [face_ref[e, pl.ds(j, 1), :] for e in range(classes + 1)]
                b_rows = [face_ref[classes + 1 + e, pl.ds(j, 1), :] for e in range(classes)]
                nexts, fluxes = [], []
                links = {}
                for e, v in picks:
                    if e < classes - 1:
                        links[e, v] = a_rows[e] * (here[e + 1, v] - here[e, v])
                    else:
                        up = pltpu.roll(here[0, v], LANES - 1, 1)
                        links[e, v] = a_rows[e] * (up - here[e, v])
                        down = pltpu.roll(here[e, v], 1, 1)
                        links[-1, v] = a_rows[classes] * (here[0, v] - down)
                for p in picks:
                    e, v = p
                    ahead = m_ref[e, j + 1, v]
                    along = b_rows[e] * (ahead - here[p])
                    m_ref[e, j, v] = ((here[p] + links[e, v]) - links[e - 1, v]) + (
                        along - before[p]
                    )
                    nexts.append(ahead)
                    fluxes.append(along)
                return nexts, fluxes

            lax.fori_loop(
                0,
                chunk_len,
                cell,
                ([first[p] for p in picks], [flux[p] for p in picks]),
                unroll=5,
            )
        return carry

    lax.fori_loop(0, ITERS, sweep, 0)

    owned = (spot >= side_pairs) & (spot < side_pairs + own) & live

    def merge(j, carry):
        for v in range(groups):
            other = pltpu.roll(m_ref[1, j, v], own, 1)
            m_ref[0, j, v] = jnp.where(owned, m_ref[0, j, v], other)
        return carry

    if classes == 2:
        lax.fori_loop(0, chunk_len, merge, 0, unroll=5)

    state_copy = pltpu.make_async_remote_copy(
        src_ref=send_ref,
        dst_ref=enter_ref,
        send_sem=send_sem,
        recv_sem=recv_sem,
        device_id={"tm": lax.min(me + 1, count - 1)},
        device_id_type=pl.DeviceIdType.MESH,
    )

    @pl.when(me == 0)
    def _():
        enter_ref[...] = jnp.zeros(enter_ref.shape, jnp.float32)

    @pl.when(me > 0)
    def _():
        state_copy.wait_recv()

    state = [enter_ref[v] for v in range(groups)]
    lane = lax.broadcasted_iota(jnp.int32, (SUB, LANES), 1)
    at_low = sub == 0
    at_high = sub == SUB - 1
    chunk_now = 0
    for start, stop in segments(width, reach, chunk_len):
        chunk = (start + reach) // chunk_len
        if chunk != chunk_now:
            state = [pltpu.roll(x, pitch, 1) for x in state]
            chunk_now = chunk
        radius = strain_ref[start // STRETCH]
        gate2 = jnp.full((SUB, LANES), jnp.where(radius >= 2, -BIG, BIG), jnp.float32)
        gate3 = jnp.full((SUB, LANES), jnp.where(radius >= 3, -BIG, BIG), jnp.float32)
        mine = lax.rem(lane + (LANES - side_pairs) + LANES - chunk * pitch, LANES) < rows

        def advance(j, x):
            wide = {v: x[v] for v in range(groups)}
            for k in range(1, 4):
                wide[-k] = jnp.where(at_low, BIG, pltpu.roll(x[groups - k], 1, 0))
                wide[groups - 1 + k] = jnp.where(at_high, BIG, pltpu.roll(x[k - 1], SUB - 1, 0))
            pair = {v: jnp.minimum(wide[v], wide[v + 1]) for v in range(-1, groups)}
            new = []
            for v in range(groups):
                near3 = jnp.minimum(pair[v - 1], pair[v])
                two = jnp.maximum(jnp.minimum(wide[v - 2], wide[v + 2]), gate2)
                three = jnp.maximum(jnp.minimum(wide[v - 3], wide[v + 3]), gate3)
                total = m_ref[0, j, v] + jnp.minimum(near3, jnp.minimum(two, three))
                if chunk == 0:
                    y_ref[j, v] = total
                else:
                    y_ref[j, v] = jnp.where(mine, total, y_ref[j, v])
                new.append(total)
            return new

        base = chunk * chunk_len - reach
        state = lax.fori_loop(start - base, stop - base, advance, state, unroll=4)

    @pl.when(me < count - 1)
    def _():
        for v in range(groups):
            send_ref[v] = pltpu.roll(state[v], (LANES - chunk_now * pitch) % LANES, 1)
        state_copy.start()

    def least(j, carry):
        low = y_ref[j, 0]
        for v in range(1, groups):
            low = jnp.minimum(low, y_ref[j, v])
        low = jnp.min(low, axis=0, keepdims=True)
        low_ref[pl.ds(j, 1), :] = low
        return carry

    lax.fori_loop(0, chunk_len, least, 0, unroll=5)

    for lag in range(L):
        sub_index, v = lag // groups, lag % groups
        cells = y_ref[0:chunk_len, v, sub_index, :] - low_ref[0:chunk_len, :]
        flat = jnp.transpose(cells)
        flat = jnp.concatenate([flat, flat[0 : 2 * SUB]], axis=0)
        for e in range(classes):
            parts = []
            for c in range(chunks):
                begin = max(reach - c * chunk_len, 0)
                end = min(width + reach - c * chunk_len, chunk_len)
                if end > begin:
                    at = c * pitch + side_pairs + e * own
                    parts.append(flat[at : at + own, begin:end])
            out_ref[lag, pl.ds(e, own, stride=classes), :] = jnp.concatenate(parts, axis=1)

    @pl.when(me < count - 1)
    def _():
        state_copy.wait_send()

    for di, dj in OFFSETS:

        @pl.when(present(di, dj))
        def _():
            halo_copy(di, dj).wait_send()


def per_device(near_trace, far_trace, inline_weight, time_weight, lag_low, lag_high, strain):
    rows, width = near_trace.shape
    reach = ITERS
    groups = L // SUB
    classes = 2
    own = rows // classes
    side_pairs = -(-reach // classes)
    pitch = -(-(rows + side_pairs) // 1)
    chunks = LANES // pitch
    chunk_len = -(-(width + 2 * reach) // chunks)
    count = lax.axis_size("tm")
    count_in = lax.axis_size("inline")

    mark = lax.broadcasted_iota(jnp.int32, (rows, width), 1)
    bounds = jnp.where(mark == 0, lag_low[:, None], lag_high[:, None])
    fields = jnp.stack(
        [
            far_trace,
            near_trace,
            inline_weight.astype(jnp.float32),
            time_weight.astype(jnp.float32),
            bounds.astype(jnp.float32),
        ]
    )
    vmem = pl.BlockSpec(memory_space=pltpu.VMEM)
    dims = (
        rows,
        width,
        reach,
        classes,
        own,
        side_pairs,
        pitch,
        chunks,
        chunk_len,
        count,
        count_in,
    )
    whole = -(-chunk_len // SUB) * SUB
    deep = -(-(chunk_len + L) // SUB) * SUB
    return pl.pallas_call(
        functools.partial(kernel, dims),
        out_shape=jax.ShapeDtypeStruct((L, rows, width), jnp.float32),
        in_specs=[vmem, pl.BlockSpec(memory_space=pltpu.SMEM)],
        out_specs=vmem,
        scratch_shapes=[
            pltpu.VMEM((9,) + fields.shape, jnp.float32),
            pltpu.VMEM((2, 3 * width, LANES), jnp.float32),
            pltpu.VMEM((classes, deep, LANES), jnp.float32),
            pltpu.VMEM((classes, whole, LANES), jnp.float32),
            pltpu.VMEM((2 * classes + 1, whole, LANES), jnp.float32),
            pltpu.VMEM((classes, chunk_len + 1, groups, SUB, LANES), jnp.float32),
            pltpu.VMEM((whole, groups, SUB, LANES), jnp.float32),
            pltpu.VMEM((whole, LANES), jnp.float32),
            pltpu.VMEM((groups, SUB, LANES), jnp.float32),
            pltpu.VMEM((groups, SUB, LANES), jnp.float32),
            pltpu.SemaphoreType.DMA((9,)),
            pltpu.SemaphoreType.DMA((9,)),
            pltpu.SemaphoreType.DMA,
            pltpu.SemaphoreType.DMA,
        ],
        compiler_params=pltpu.CompilerParams(collective_id=0, has_side_effects=True),
    )(fields, strain)


def solution(mesh):
    return jax.shard_map(
        per_device,
        mesh=mesh,
        in_specs=(
            P(("group", "inline"), "tm"),
            P(("group", "inline"), "tm"),
            P(("group", "inline"), "tm"),
            P(("group", "inline"), "tm"),
            P(("group", "inline")),
            P(("group", "inline")),
            P(("group", "tm")),
        ),
        out_specs=P(None, ("group", "inline"), "tm"),
        check_vma=False,
    )
```

time: 82.2 us -> 45 us (0.55)
  Pallas kernels: 59 us -> 39.3 us
  starting transfers between devices: 8.37 us -> 0 us
  waiting for transfers between devices: 4.91 us -> 0 us
  other arithmetic: 3.78 us -> 0.08 us
    pallas_call x1, Pallas kernels: 59 us -> 39.3 us  [per_device(): pl.pallas_call(functools.partial(kernel, dims), out_shape=jax.ShapeDtypeS...]
    ppermute x4 -> x0, starting transfers between devices: 8.37 us -> none  [the longest x1 3.2 us: per_device(): lax.ppermute(wide[:, rows - reach:], 'inline', [(i, i + 1) for i in range...]
    ppermute x4 -> x0, waiting for transfers between devices: 4.91 us -> none  [the longest x1 3.72 us: per_device(): lax.ppermute(wide[:, :reach], 'inline', [(i + 1, i) for i in range(count_...]
    transpose x4 -> x0, other arithmetic: 2.79 us -> none  [packed(): return jnp.transpose(lanes)]
    unnamed x17 -> x15, local copies, waits for them, and re-layouts: 3.74 us -> 5.26 us
    slice x13 -> x0, local copies, waits for them, and re-layouts: 1.07 us -> none  [the longest x2 0.67 us: per_device(): far_p = packed(wide[0], chunk_len + L)]
  transfers between devices with their start and end apart: 4 -> 0, of which waited for: 3 -> 0; matrix products, arithmetic and copies ran while one was open for 0% -> 0% of each run, Pallas kernels for 0% -> 0%
where the time goes in v1:
time: 45 us; the launch traced here: 44.6 us
  Pallas kernels  39.3 us (87%)
  local copies, waits for them, and re-layouts  5.26 us (12%)
    pallas_call x1, Pallas kernels, per_device(): pl.pallas_call(functools.partial(kernel, dims), out_shape=jax.ShapeDtypeS...  39.3 us
    unnamed x15, local copies, waits for them, and re-layouts  5.26 us

profile of v1, /device:TPU:5, one launch (start us, length us, event | category | flops | bytes accessed | tf_op | source)
XLA Modules:
  0.0 44.6 jit_solution(3398796521359589406)
XLA Ops:
  0.0 0.0 copy-start.1
  0.0 0.7 %constant_dynamic-update-slice_fusion.4 = f32[5,16,128]{2,1,0:T(8,128)S(1)} fusion(f32[16,128]{1,0:T(8,128)} %param.8), kind=kLoop, calls=%fused_computation.4 | loop fusion | bytes 16384
  0.7 0.0 copy-done.1
  0.7 0.0 copy-start.2
  0.7 0.7 %copy-done.2 = s32[16,128]{1,0:T(8,128)S(1)} copy-done((s32[16,128]{1,0:T(8,128)S(1)}, s32[16,128]{1,0:T(8,128)}, u32[]{:S(2)}) %copy-start.2) | copy-done | bytes 8216
  1.4 0.0 copy-start.3
  1.4 0.7 %copy-done.3 = s32[16,128]{1,0:T(8,128)S(1)} copy-done((s32[16,128]{1,0:T(8,128)S(1)}, s32[16,128]{1,0:T(8,128)}, u32[]{:S(2)}) %copy-start.3) | copy-done | bytes 8216
  2.1 0.0 copy-start.4
  2.1 0.0 copy-start.5
  2.1 0.6 %copy-done.4 = s32[16]{0:T(128)S(1)} copy-done((s32[16]{0:T(128)S(1)}, s32[16]{0:T(128)}, u32[]{:S(2)}) %copy-start.4) | copy-done | bytes 88
  2.8 0.0 copy-done.5
  2.8 0.1 constant_dynamic-update-slice_fusion.fields_ref
  2.9 0.0 copy-start
  2.9 0.6 %copy-done = f32[5,16,128]{2,1,0:T(8,128)} copy-done((f32[5,16,128]{2,1,0:T(8,128)}, f32[5,16,128]{2,1,0:T(8,128)S(1)}, u32[]{:S(2)}) %copy-start) | copy-done | bytes 40984
  3.5 39.3 %shard_map.73 = f32[64,16,128]{2,1,0:T(8,128)} custom-call(f32[5,16,128]{2,1,0:T(8,128)} %copy-done, s32[2]{0:T(128)} %strain_ref.1), custom_call_target="tpu_custom_call" | custom-call | tf_op jit(solution)/shard_map/pallas_call | solution.py:410
  42.8 1.9 %copy.13 = f32[64,16,128]{2,1,0:T(8,128)} copy(f32[64,16,128]{2,1,0:T(8,128)} %shard_map.73) | data formatting | bytes 1048576
  (4 shorter events, 0.0 us)
Async XLA Ops:
  0.0 0.7 %copy-start.1 = (f32[16,128]{1,0:T(8,128)S(1)}, f32[16,128]{1,0:T(8,128)}, u32[]{:S(2)}) copy-start(f32[16,128]{1,0:T(8,128)} %param.7) | copy-start | bytes 24580
  0.7 0.7 %copy-start.2 = (s32[16,128]{1,0:T(8,128)S(1)}, s32[16,128]{1,0:T(8,128)}, u32[]{:S(2)}) copy-start(s32[16,128]{1,0:T(8,128)} %param.9) | copy-start | bytes 24580
  1.4 0.7 %copy-start.3 = (s32[16,128]{1,0:T(8,128)S(1)}, s32[16,128]{1,0:T(8,128)}, u32[]{:S(2)}) copy-start(s32[16,128]{1,0:T(8,128)} %param.10) | copy-start | bytes 24580
  2.1 0.7 %copy-start.4 = (s32[16]{0:T(128)S(1)}, s32[16]{0:T(128)}, u32[]{:S(2)}) copy-start(s32[16]{0:T(128)} %param.12) | copy-start | bytes 196
  2.1 0.7 %copy-start.5 = (s32[16]{0:T(128)S(1)}, s32[16]{0:T(128)}, u32[]{:S(2)}) copy-start(s32[16]{0:T(128)} %param.11) | copy-start | bytes 196
  2.9 0.6 %copy-start = (f32[5,16,128]{2,1,0:T(8,128)}, f32[5,16,128]{2,1,0:T(8,128)S(1)}, u32[]{:S(2)}) copy-start(f32[5,16,128]{2,1,0:T(8,128)S(1)} %constant_dynamic-update-slice_fusion.fields_ref) | copy-start | bytes 122884

commit v2 on v1

--- a/solution.py
+++ b/solution.py
@@ -254,7 +254,7 @@
                 chunk_len,
                 cell,
                 ([first[p] for p in picks], [flux[p] for p in picks]),
-                unroll=5,
+                unroll=chunk_len,
             )
         return carry
 
@@ -323,7 +323,7 @@
             return new
 
         base = chunk * chunk_len - reach
-        state = lax.fori_loop(start - base, stop - base, advance, state, unroll=4)
+        state = lax.fori_loop(start - base, stop - base, advance, state, unroll=stop - start)
 
     @pl.when(me < count - 1)
     def _():

time: 45 us -> 36.8 us (0.82)
  Pallas kernels: 39.3 us -> 31.1 us
    pallas_call x1, Pallas kernels: 39.3 us -> 31.1 us  [per_device(): pl.pallas_call(functools.partial(kernel, dims), out_shape=jax.ShapeDtypeS...]
where the time goes in v2:
time: 36.8 us; the launch traced here: 36.4 us
  Pallas kernels  31.1 us (85%)
  local copies, waits for them, and re-layouts  5.26 us (14%)
    pallas_call x1, Pallas kernels, per_device(): pl.pallas_call(functools.partial(kernel, dims), out_shape=jax.ShapeDtypeS...  31.1 us
    unnamed x15, local copies, waits for them, and re-layouts  5.26 us

profile of v2, /device:TPU:5, one launch (start us, length us, event | category | flops | bytes accessed | tf_op | source)
XLA Modules:
  0.0 36.4 jit_solution(17631001632019964233)
XLA Ops:
  0.0 0.0 copy-start.1
  0.0 0.7 %constant_dynamic-update-slice_fusion.4 = f32[5,16,128]{2,1,0:T(8,128)S(1)} fusion(f32[16,128]{1,0:T(8,128)} %param.8), kind=kLoop, calls=%fused_computation.4 | loop fusion | bytes 16384
  0.7 0.0 copy-done.1
  0.7 0.0 copy-start.2
  0.7 0.7 %copy-done.2 = s32[16,128]{1,0:T(8,128)S(1)} copy-done((s32[16,128]{1,0:T(8,128)S(1)}, s32[16,128]{1,0:T(8,128)}, u32[]{:S(2)}) %copy-start.2) | copy-done | bytes 8216
  1.4 0.0 copy-start.3
  1.4 0.7 %copy-done.3 = s32[16,128]{1,0:T(8,128)S(1)} copy-done((s32[16,128]{1,0:T(8,128)S(1)}, s32[16,128]{1,0:T(8,128)}, u32[]{:S(2)}) %copy-start.3) | copy-done | bytes 8216
  2.1 0.0 copy-start.4
  2.1 0.0 copy-start.5
  2.1 0.6 %copy-done.4 = s32[16]{0:T(128)S(1)} copy-done((s32[16]{0:T(128)S(1)}, s32[16]{0:T(128)}, u32[]{:S(2)}) %copy-start.4) | copy-done | bytes 88
  2.8 0.0 copy-done.5
  2.8 0.1 constant_dynamic-update-slice_fusion.fields_ref
  2.9 0.0 copy-start
  2.9 0.6 %copy-done = f32[5,16,128]{2,1,0:T(8,128)} copy-done((f32[5,16,128]{2,1,0:T(8,128)}, f32[5,16,128]{2,1,0:T(8,128)S(1)}, u32[]{:S(2)}) %copy-start) | copy-done | bytes 40984
  3.5 31.1 %shard_map.73 = f32[64,16,128]{2,1,0:T(8,128)} custom-call(f32[5,16,128]{2,1,0:T(8,128)} %copy-done, s32[2]{0:T(128)} %strain_ref.1), custom_call_target="tpu_custom_call" | custom-call | tf_op jit(solution)/shard_map/pallas_call | solution.py:410
  34.5 1.9 %copy.13 = f32[64,16,128]{2,1,0:T(8,128)} copy(f32[64,16,128]{2,1,0:T(8,128)} %shard_map.73) | data formatting | bytes 1048576
  (4 shorter events, 0.0 us)
Async XLA Ops:
  0.0 0.7 %copy-start.1 = (f32[16,128]{1,0:T(8,128)S(1)}, f32[16,128]{1,0:T(8,128)}, u32[]{:S(2)}) copy-start(f32[16,128]{1,0:T(8,128)} %param.7) | copy-start | bytes 24580
  0.7 0.7 %copy-start.2 = (s32[16,128]{1,0:T(8,128)S(1)}, s32[16,128]{1,0:T(8,128)}, u32[]{:S(2)}) copy-start(s32[16,128]{1,0:T(8,128)} %param.9) | copy-start | bytes 24580
  1.4 0.7 %copy-start.3 = (s32[16,128]{1,0:T(8,128)S(1)}, s32[16,128]{1,0:T(8,128)}, u32[]{:S(2)}) copy-start(s32[16,128]{1,0:T(8,128)} %param.10) | copy-start | bytes 24580
  2.1 0.7 %copy-start.4 = (s32[16]{0:T(128)S(1)}, s32[16]{0:T(128)}, u32[]{:S(2)}) copy-start(s32[16]{0:T(128)} %param.12) | copy-start | bytes 196
  2.1 0.7 %copy-start.5 = (s32[16]{0:T(128)S(1)}, s32[16]{0:T(128)}, u32[]{:S(2)}) copy-start(s32[16]{0:T(128)} %param.11) | copy-start | bytes 196
  2.9 0.6 %copy-start = (f32[5,16,128]{2,1,0:T(8,128)}, f32[5,16,128]{2,1,0:T(8,128)S(1)}, u32[]{:S(2)}) copy-start(f32[5,16,128]{2,1,0:T(8,128)S(1)} %constant_dynamic-update-slice_fusion.fields_ref) | copy-start | bytes 122884

commit v3 on v2

--- a/solution.py
+++ b/solution.py
@@ -36,10 +36,17 @@
 
 def kernel(
     dims,
-    fields_ref,
+    far_in,
+    near_in,
+    inline_in,
+    time_in,
+    bounds_in,
     strain_ref,
     out_ref,
-    recv_ref,
+    trace_ref,
+    weight_ref,
+    trace_recv,
+    weight_recv,
     time_ref,
     far_ref,
     near_ref,
@@ -49,6 +56,7 @@
     low_ref,
     send_ref,
     enter_ref,
+    local_sems,
     send_sems,
     recv_sems,
     send_sem,
@@ -74,6 +82,21 @@
             "tm": lax.clamp(0, me + dj, count - 1),
         }
 
+    local = [
+        pltpu.make_async_copy(source, target, local_sems.at[k])
+        for k, (source, target) in enumerate(
+            (
+                (far_in, trace_ref.at[0]),
+                (near_in, trace_ref.at[1]),
+                (inline_in, weight_ref.at[0]),
+                (time_in, weight_ref.at[1]),
+                (bounds_in, weight_ref.at[2]),
+            )
+        )
+    ]
+    for copy in local:
+        copy.start()
+
     barrier = pltpu.get_barrier_semaphore()
     for di, dj in OFFSETS:
 
@@ -89,32 +112,43 @@
     ]
     pl.semaphore_wait(barrier, beside[0] * beside[1] - 1)
 
-    def halo_copy(di, dj):
+    def halo_copies(di, dj):
         target = slot_of(-di, -dj)
-        return pltpu.make_async_remote_copy(
-            src_ref=fields_ref,
-            dst_ref=recv_ref.at[target],
-            send_sem=send_sems.at[slot_of(di, dj)],
-            recv_sem=recv_sems.at[target],
-            device_id=device(di, dj),
-            device_id_type=pl.DeviceIdType.MESH,
-        )
+        return [
+            pltpu.make_async_remote_copy(
+                src_ref=source,
+                dst_ref=landing.at[target],
+                send_sem=send_sems.at[kind, slot_of(di, dj)],
+                recv_sem=recv_sems.at[kind, target],
+                device_id=device(di, dj),
+                device_id_type=pl.DeviceIdType.MESH,
+            )
+            for kind, (source, landing) in enumerate(
+                ((trace_ref, trace_recv), (weight_ref, weight_recv))
+            )
+        ]
+
+    for copy in local:
+        copy.wait()
 
     for di, dj in OFFSETS:
 
         @pl.when(present(di, dj))
         def _():
-            halo_copy(di, dj).start()
+            for copy in halo_copies(di, dj):
+                copy.start()
 
         @pl.when(jnp.logical_not(present(di, dj)))
         def _():
-            recv_ref[slot_of(di, dj)] = jnp.zeros(fields_ref.shape, jnp.float32)
+            trace_recv[slot_of(di, dj)] = jnp.zeros(trace_ref.shape, jnp.float32)
+            weight_recv[slot_of(di, dj)] = jnp.zeros(weight_ref.shape, jnp.int32)
 
     for di, dj in OFFSETS:
 
         @pl.when(present(di, dj))
         def _():
-            halo_copy(-di, -dj).wait_recv()
+            for copy in halo_copies(-di, -dj):
+                copy.wait_recv()
 
     stacked = 3 * own
 
@@ -122,10 +156,12 @@
         parts = []
         for di in (-1, 0, 1):
             pick = pl.ds(parity, own, stride=classes)
+            own_ref, landing = (trace_ref, trace_recv) if field < 2 else (weight_ref, weight_recv)
             if di == 0 and dj == 0:
-                parts.append(fields_ref[field, pick, :])
+                cells = own_ref[field % 2 if field < 4 else 2, pick, :]
             else:
-                parts.append(recv_ref[slot_of(di, dj), field, pick, :])
+                cells = landing[slot_of(di, dj), field % 2 if field < 4 else 2, pick, :]
+            parts.append(cells.astype(jnp.float32))
         return parts
 
     for pair in range(2):
@@ -364,7 +400,8 @@
 
         @pl.when(present(di, dj))
         def _():
-            halo_copy(di, dj).wait_send()
+            for copy in halo_copies(di, dj):
+                copy.wait_send()
 
 
 def per_device(near_trace, far_trace, inline_weight, time_weight, lag_low, lag_high, strain):
@@ -382,15 +419,6 @@
 
     mark = lax.broadcasted_iota(jnp.int32, (rows, width), 1)
     bounds = jnp.where(mark == 0, lag_low[:, None], lag_high[:, None])
-    fields = jnp.stack(
-        [
-            far_trace,
-            near_trace,
-            inline_weight.astype(jnp.float32),
-            time_weight.astype(jnp.float32),
-            bounds.astype(jnp.float32),
-        ]
-    )
     vmem = pl.BlockSpec(memory_space=pltpu.VMEM)
     dims = (
         rows,
@@ -410,10 +438,14 @@
     return pl.pallas_call(
         functools.partial(kernel, dims),
         out_shape=jax.ShapeDtypeStruct((L, rows, width), jnp.float32),
-        in_specs=[vmem, pl.BlockSpec(memory_space=pltpu.SMEM)],
+        in_specs=[pl.BlockSpec(memory_space=pl.ANY)] * 5
+        + [pl.BlockSpec(memory_space=pltpu.SMEM)],
         out_specs=vmem,
         scratch_shapes=[
-            pltpu.VMEM((9,) + fields.shape, jnp.float32),
+            pltpu.VMEM((2, rows, width), jnp.float32),
+            pltpu.VMEM((3, rows, width), jnp.int32),
+            pltpu.VMEM((9, 2, rows, width), jnp.float32),
+            pltpu.VMEM((9, 3, rows, width), jnp.int32),
             pltpu.VMEM((2, 3 * width, LANES), jnp.float32),
             pltpu.VMEM((classes, deep, LANES), jnp.float32),
             pltpu.VMEM((classes, whole, LANES), jnp.float32),
@@ -423,13 +455,14 @@
             pltpu.VMEM((whole, LANES), jnp.float32),
             pltpu.VMEM((groups, SUB, LANES), jnp.float32),
             pltpu.VMEM((groups, SUB, LANES), jnp.float32),
-            pltpu.SemaphoreType.DMA((9,)),
-            pltpu.SemaphoreType.DMA((9,)),
+            pltpu.SemaphoreType.DMA((5,)),
+            pltpu.SemaphoreType.DMA((2, 9)),
+            pltpu.SemaphoreType.DMA((2, 9)),
             pltpu.SemaphoreType.DMA,
             pltpu.SemaphoreType.DMA,
         ],
         compiler_params=pltpu.CompilerParams(collective_id=0, has_side_effects=True),
-    )(fields, strain)
+    )(far_trace, near_trace, inline_weight, time_weight, bounds, strain)
 
 
 def solution(mesh):

time: 36.8 us -> 34.6 us (0.940)
  local copies, waits for them, and re-layouts: 5.26 us -> 2.53 us
  other arithmetic: 0.08 us -> 0.67 us
    unnamed x15 -> x5, local copies, waits for them, and re-layouts: 5.26 us -> 2.53 us
    select_n x0 -> x1, other arithmetic: none -> 0.67 us  [per_device(): bounds = jnp.where(mark == 0, lag_low[:, None], lag_high[:, None])]
where the time goes in v3:
time: 34.6 us; the launch traced here: 34.4 us
  Pallas kernels  31.1 us (90%)
  local copies, waits for them, and re-layouts  2.53 us (7%)
  other arithmetic  0.67 us (2%)
    pallas_call x1, Pallas kernels, per_device(): pl.pallas_call(functools.partial(kernel, dims), out_shape=jax.ShapeDtypeS...  31.1 us
    unnamed x5, local copies, waits for them, and re-layouts  2.53 us

profile of v3, /device:TPU:5, one launch (start us, length us, event | category | flops | bytes accessed | tf_op | source)
XLA Modules:
  0.0 34.4 jit_solution(9471891749458498233)
XLA Ops:
  0.0 0.0 copy-start
  0.0 0.0 copy-start.1
  0.0 0.6 %copy-done = s32[16]{0:T(128)S(1)} copy-done((s32[16]{0:T(128)S(1)}, s32[16]{0:T(128)}, u32[]{:S(2)}) %copy-start) | copy-done | bytes 88
  0.7 0.0 copy-done.1
  0.7 0.7 %broadcast_select_fusion.bounds_in = s32[16,128]{1,0:T(8,128)} fusion(s32[16]{0:T(128)S(1)} %copy-done, s32[16]{0:T(128)S(1)} %copy-done.1, pred[128]{0:T(512)(128)(4,1)S(1)} %iota_compare_fusion), kind=kLoop, calls=%fused_computation | loop fusion | flops 2048 | bytes 8448 | tf_op jit(solution)/shard_map/jit(_where)/select_n | solution.py:421
  1.3 31.1 %shard_map.73 = f32[64,16,128]{2,1,0:T(8,128)} custom-call(f32[16,128]{1,0:T(8,128)} %far_in.1, f32[16,128]{1,0:T(8,128)} %near_in.1, s32[16,128]{1,0:T(8,128)} %inline_in.1, s32[16,128]{1,0:T(8,128)} %time_in.1, s32[16,128]{1,0:T(8,128)} %broadcast_select_fusion.bounds_in, s32[2]{0:T(128)} %strain_ref.1), custom_call_target="tpu_custom_call" | custom-call | tf_op jit(solution)/shard_map/pallas_call | solution.py:438
  32.5 1.9 %copy.9 = f32[64,16,128]{2,1,0:T(8,128)} copy(f32[64,16,128]{2,1,0:T(8,128)} %shard_map.73) | data formatting | bytes 1048576
  (1 shorter events, 0.0 us)
Async XLA Ops:
  0.0 0.7 %copy-start = (s32[16]{0:T(128)S(1)}, s32[16]{0:T(128)}, u32[]{:S(2)}) copy-start(s32[16]{0:T(128)} %param.12) | copy-start | bytes 196
  0.0 0.7 %copy-start.1 = (s32[16]{0:T(128)S(1)}, s32[16]{0:T(128)}, u32[]{:S(2)}) copy-start(s32[16]{0:T(128)} %param.11) | copy-start | bytes 196
